TPU v7x, 512 devices: a whole 4x4x16 slice. The times are simulated.
512 devices in a mesh: row: 8 (over x, core), col: 16 (over z), layer: 4 (over y).
Axes of the slice: x: 4, y: 4, z: 16, core: 2. Of those that a mesh axis runs over, the one named last changes fastest.
Arguments:
- occurrences: bfloat16 [8192, 10240], P(('row', 'col', 'layer')), may hold values from -6 to 6
- idf_weight: float32 [8192], P(('row', 'col', 'layer')), may hold values from 0.25 to 2
- pattern: int32 [64, 80], replicated, may hold values 0 or 1
Outputs:
- margin: bfloat16 [10240, 10240], P('row', 'col')
All inputs are finite; a program needn't handle non-finite values.
Results may differ from a plain program's by a relative error of at most 0.0058.
Values may be sent and summed in bfloat16 or wider, within the bound.
No kernel may reach another device: no remote copies, remote signals or barrier semaphores. Data moves between devices by JAX's collectives and lax.ppermute only.
A program may use at most 64 MiB of HBM per device.

v0:
```python
import math
import jax
import jax.numpy as jnp
from jax import lax
from jax.sharding import PartitionSpec as P


def finish(partial_rows, row_start, col_start, factor):
    row_ids = row_start + lax.broadcasted_iota(jnp.int32, partial_rows.shape, 0)
    col_ids = col_start + lax.broadcasted_iota(jnp.int32, partial_rows.shape, 1)
    result = jnp.where(row_ids == col_ids, jnp.float32(0.0), partial_rows * factor)
    return result.astype(jnp.bfloat16)


def body(occurrences, idf_weight, pattern):
    owned, reads = occurrences.shape
    n_rows = lax.axis_size("row")
    n_cols = lax.axis_size("col")
    n_layers = lax.axis_size("layer")
    factor = 1.0 / math.sqrt(owned * n_rows * n_cols * n_layers)
    owner = lax.axis_index(("row", "col", "layer"))
    block_row = owner * owned // 128
    flags = lax.dynamic_slice_in_dim(pattern, block_row, 1, 0)[0]
    read_mask = jnp.repeat(flags.astype(jnp.float32), 128)
    weighted = (occurrences.astype(jnp.float32) * idf_weight[:, None] * read_mask[None, :]).astype(
        jnp.bfloat16
    )
    piece_len = reads // (n_rows * n_cols)
    reordered = (
        weighted.reshape(owned, n_cols, n_rows, piece_len)
        .transpose(0, 2, 1, 3)
        .reshape(owned, reads)
    )
    row_part, col_part = (
        lax.all_to_all(weighted, ("row", "col"), split_axis=1, concat_axis=0, tiled=True),
        lax.all_to_all(reordered, ("row", "col"), split_axis=1, concat_axis=0, tiled=True),
    )
    column_reads = lax.all_gather(col_part, "row", axis=1, tiled=True)
    partial_tile = lax.dot_general(
        lax.all_gather(row_part, "col", axis=1, tiled=True),
        column_reads,
        (((0,), (0,)), ((), ())),
        preferred_element_type=jnp.float32,
    )
    row_count = partial_tile.shape[0]
    row_start = lax.axis_index("row") * row_count
    col_start = lax.axis_index("col") * partial_tile.shape[1]
    total = lax.psum(partial_tile, "layer")
    return finish(total, row_start, col_start, factor)


def solution(mesh):
    placed = (P(("row", "col", "layer"), None), P(("row", "col", "layer")), P())
    return jax.shard_map(
        body, mesh=mesh, in_specs=placed, out_specs=P("row", "col"), check_vma=False
    )
```

profile of v0, /device:TPU:1, one launch (start us, length us, event | category | flops | bytes accessed | tf_op | source)
XLA Modules:
  0.0 287.5 jit_solution(10885676402827663510)
XLA Ops:
  6.5 0.0 all-gather.5.cloned.1.call-start
  6.5 0.7 convert_bitcast_fusion
  7.2 0.1 broadcast_bitcast_fusion
  7.3 1.1 multiply_convert_fusion
  8.4 0.6 reshape.14
  9.1 0.1 copy.9
  9.2 0.3 copy.10
  9.6 52.5 %all_to_all.38 = bf16[16,128,80]{2,0,1:T(8,128)(2,1)S(1)} all-to-all(bf16[16,128,80]{2,0,1:T(8,128)(2,1)S(1)} %copy.10), channel_id=1, replica_groups=mesh['row'=8,'col'=16,'layer'=4] {'row','col'}, dimensions={1} | all-to-all | bytes 655360 | tf_op jit(solution)/shard_map/all_to_all | solution.py:36
  62.0 0.9 copy.11
  63.0 0.0 all-gather.5.cloned.1.call-update
  63.0 0.0 all-gather.3.cloned.1.call-start
  63.0 0.6 all_to_all.28
  63.7 0.3 copy.7
  64.0 39.7 %all_to_all.39 = bf16[16,128,80]{2,0,1:T(8,128)(2,1)S(1)} all-to-all(bf16[16,128,80]{2,0,1:T(8,128)(2,1)S(1)} %copy.7), channel_id=1, replica_groups=mesh['row'=8,'col'=16,'layer'=4] {'row','col'}, dimensions={1} | all-to-all | bytes 655360 | tf_op jit(solution)/shard_map/all_to_all | solution.py:35
  103.8 0.9 copy.8
  104.7 0.0 all-gather.3.cloned.1.call-update
  104.7 0.0 all-reduce.2.cloned.1.call-start
  104.8 0.0 all-gather.5.cloned.1.call-done
  104.8 67.3 %all-gather.3.cloned.1.call-done = bf16[2048,1280]{0,1:T(8,128)(2,1)} async-done(((bf16[2048,80]{0,1:T(8,128)(2,1)}), bf16[2048,1280]{0,1:T(8,128)(2,1)}) %all-gather.3.cloned.1.call-update) | async-done | bytes 5242896 | tf_op jit(solution)/shard_map/all_gather | solution.py:40
  172.1 9.3 %fusion = f32[1280,640]{1,0:T(8,128)} fusion(bf16[2048,1280]{0,1:T(8,128)(2,1)} %all-gather.3.cloned.1.call-done, bf16[2048,640]{0,1:T(8,128)(2,1)} %all-gather.5.cloned.1.call-done), kind=kOutput, calls=%fused_computation.6 | convolution fusion | flops 3355443200 | bytes 11141120 | tf_op jit(solution)/shard_map/dot_general | solution.py:39
  181.3 0.0 all-reduce.2.cloned.1.call-update
  181.4 96.0 %all-reduce.2.cloned.1.call-done = f32[1280,640]{1,0:T(8,128)} async-done(((f32[1280,640]{1,0:T(8,128)}), f32[1280,640]{1,0:T(8,128)}) %all-reduce.2.cloned.1.call-update) | async-done | bytes 3276816 | tf_op jit(solution)/shard_map/psum | solution.py:48
  277.4 3.5 %select_convert_fusion = bf16[1280,640]{1,0:T(8,128)(2,1)} fusion(f32[1280,640]{1,0:T(8,128)} %all-reduce.2.cloned.1.call-done, s32[640]{0:T(1024)S(1)} %iota_add_fusion.1, s32[1280]{0:T(1024)S(1)} %iota_add_fusion), kind=kLoop, calls=%fused_computation | loop fusion | flops 3276800 | bytes 4922880 | tf_op jit(solution)/shard_map/convert_element_type | solution.py:12
  (2 shorter events, 0.0 us)
Async XLA Ops:
  6.5 98.3 %all-gather.5.cloned.1.call-start = ((), (), s32[]{:S(2)}) async-start(), calls=%async_computation.3 | async-start | bytes 2949120 | tf_op jit(solution)/shard_map/all_gather | solution.py:38
  63.0 109.1 %all-gather.3.cloned.1.call-start = ((), (), s32[]{:S(2)}) async-start(), calls=%async_computation.2 | async-start | bytes 5570560 | tf_op jit(solution)/shard_map/all_gather | solution.py:40
  104.7 172.7 %all-reduce.2.cloned.1.call-start = ((), (), s32[]{:S(2)}) async-start(), calls=%async_computation.4 | async-start | bytes 6553600 | tf_op jit(solution)/shard_map/psum | solution.py:48
Sparse Core Ops, SparseCore 0:
  63.1 29.0 all-gather.4
  104.9 67.1 all-gather.2
  181.5 95.8 all-reduce.1
where the time goes:
time: 288 us; the launch traced here: 287 us
  waiting for transfers between devices  163 us (57%)
  blocking collectives  92.2 us (32%)
  between operations  13.2 us (5%)
  matrix products  9.28 us (3%)
  other arithmetic  5.36 us (2%)
  local copies, waits for them, and re-layouts  4.02 us (1%)
    psum x1, waiting for transfers between devices, body(): total = lax.psum(partial_tile, 'layer')  96 us
    all_gather x1, waiting for transfers between devices, body(): lax.all_gather(row_part, 'col', axis=1, tiled=True)  67.3 us
    all_to_all x1, blocking collectives, body(): lax.all_to_all(reordered, ('row', 'col'), split_axis=1, concat_axis=0, ti...  52.5 us
    all_to_all x1, blocking collectives, body(): lax.all_to_all(weighted, ('row', 'col'), split_axis=1, concat_axis=0, til...  39.7 us
    dot_general x1, matrix products, body(): lax.dot_general(lax.all_gather(row_part, 'col', axis=1, tiled=True), colu...  9.28 us
  transfers between devices with their start and end apart: 3, of which 2 were waited for; matrix products, arithmetic and copies ran while one was open for 0% of the time, Pallas kernels for 0%

commit v1 on v0

--- a/solution.py
+++ b/solution.py
@@ -3,6 +3,24 @@
 import jax.numpy as jnp
 from jax import lax
 from jax.sharding import PartitionSpec as P
+
+
+def ring_gather(array, axis, dim):
+    ways, here, step = (lax.axis_size(axis), lax.axis_index(axis), array.shape[dim])
+    lengths = [n * ways if d == dim else n for d, n in enumerate(array.shape)]
+    full = lax.dynamic_update_slice_in_dim(
+        jnp.zeros(lengths, array.dtype), array, here * step, axis=dim
+    )
+    going_up = going_down = array
+    for far in range(1, ways // 2 + 1):
+        going_up = lax.ppermute(going_up, axis, [(d, (d + 1) % ways) for d in range(ways)])
+        full = lax.dynamic_update_slice_in_dim(full, going_up, (here - far) % ways * step, axis=dim)
+        if 2 * far < ways:
+            going_down = lax.ppermute(going_down, axis, [(d, (d - 1) % ways) for d in range(ways)])
+            full = lax.dynamic_update_slice_in_dim(
+                full, going_down, (here + far) % ways * step, axis=dim
+            )
+    return full
 
 
 def finish(partial_rows, row_start, col_start, factor):
@@ -37,7 +55,7 @@
     )
     column_reads = lax.all_gather(col_part, "row", axis=1, tiled=True)
     partial_tile = lax.dot_general(
-        lax.all_gather(row_part, "col", axis=1, tiled=True),
+        ring_gather(row_part, "col", 1),
         column_reads,
         (((0,), (0,)), ((), ())),
         preferred_element_type=jnp.float32,

time: 288 us -> 429 us (1.49)
  local copies, waits for them, and re-layouts: 4.02 us -> 109 us
  starting transfers between devices: 0.09 us -> 47.3 us
  waiting for transfers between devices: 163 us -> 149 us
    dynamic_update_slice x0 -> x16, local copies, waits for them, and re-layouts: none -> 103 us  [the longest x8 51.3 us: ring_gather(): lax.dynamic_update_slice_in_dim(full, going_up, (here - far) % ways * ste...]
    all_gather x1 -> x0, waiting for transfers between devices: 67.3 us -> none  [body(): lax.all_gather(row_part, 'col', axis=1, tiled=True)]
    ppermute x0 -> x15, waiting for transfers between devices: none -> 52.4 us  [the longest x8 52.4 us: ring_gather(): lax.ppermute(going_up, axis, [(d, (d + 1) % ways) for d in range(ways)])]
    ppermute x0 -> x15, starting transfers between devices: none -> 47.3 us  [the longest x7 28 us: ring_gather(): lax.ppermute(going_down, axis, [(d, (d - 1) % ways) for d in range(ways)])]
  transfers between devices with their start and end apart: 3 -> 17, of which waited for: 2 -> 8; matrix products, arithmetic and copies ran while one was open for 0% -> 25% of each run, Pallas kernels for 0% -> 0%
where the time goes in v1:
time: 429 us; the launch traced here: 426 us
  waiting for transfers between devices  149 us (35%)
  local copies, waits for them, and re-layouts  109 us (25%)
  blocking collectives  92.2 us (21%)
  starting transfers between devices  47.3 us (11%)
  between operations  14 us (3%)
  matrix products  9.33 us (2%)
  other arithmetic  5.36 us (1%)
    psum x1, waiting for transfers between devices, body(): total = lax.psum(partial_tile, 'layer')  96.1 us
    all_to_all x1, blocking collectives, body(): lax.all_to_all(reordered, ('row', 'col'), split_axis=1, concat_axis=0, ti...  52.5 us
    ppermute x8, waiting for transfers between devices, ring_gather(): lax.ppermute(going_up, axis, [(d, (d + 1) % ways) for d in range(ways)])  52.4 us
    dynamic_update_slice x8, local copies, waits for them, and re-layouts, ring_gather(): lax.dynamic_update_slice_in_dim(full, going_up, (here - far) % ways * ste...  51.3 us
    dynamic_update_slice x7, local copies, waits for them, and re-layouts, ring_gather(): lax.dynamic_update_slice_in_dim(full, going_down, (here + far) % ways * s...  46.3 us
    all_to_all x1, blocking collectives, body(): lax.all_to_all(weighted, ('row', 'col'), split_axis=1, concat_axis=0, til...  39.7 us
    ppermute x7, starting transfers between devices, ring_gather(): lax.ppermute(going_down, axis, [(d, (d - 1) % ways) for d in range(ways)])  28 us
    ppermute x8, starting transfers between devices, ring_gather(): lax.ppermute(going_up, axis, [(d, (d + 1) % ways) for d in range(ways)])  19.3 us
  transfers between devices with their start and end apart: 17, of which 8 were waited for; matrix products, arithmetic and copies ran while one was open for 25% of the time, Pallas kernels for 0%

profile of v1, /device:TPU:1, one launch (start us, length us, event | category | flops | bytes accessed | tf_op | source)
XLA Modules:
  0.0 425.8 jit_solution(7443391282822093595)
XLA Ops:
  9.6 52.5 %all_to_all.38 = bf16[16,128,80]{2,0,1:T(8,128)(2,1)S(1)} all-to-all(bf16[16,128,80]{2,0,1:T(8,128)(2,1)S(1)} %copy.9), channel_id=1, replica_groups=mesh['row'=8,'col'=16,'layer'=4] {'row','col'}, dimensions={1} | all-to-all | bytes 655360 | tf_op jit(solution)/shard_map/all_to_all | solution.py:54
  64.0 39.7 %all_to_all.39 = bf16[16,128,80]{2,0,1:T(8,128)(2,1)S(1)} all-to-all(bf16[16,128,80]{2,0,1:T(8,128)(2,1)S(1)} %copy.7), channel_id=1, replica_groups=mesh['row'=8,'col'=16,'layer'=4] {'row','col'}, dimensions={1} | all-to-all | bytes 655360 | tf_op jit(solution)/shard_map/all_to_all | solution.py:53
  110.3 10.2 %collective-permute-done = bf16[2048,80]{1,0:T(8,128)(2,1)S(1)} collective-permute-done((bf16[2048,80]{1,0:T(8,128)(2,1)S(1)}, bf16[2048,80]{1,0:T(8,128)(2,1)S(1)}, u32[]{:S(2)}, u32[]{:S(2)}) %collective-permute-start) | collective-permute-done | bytes 327712 | tf_op jit(solution)/shard_map/ppermute | solution.py:16
  127.0 9.3 %collective-permute-done.2 = bf16[2048,80]{1,0:T(8,128)(2,1)S(1)} collective-permute-done((bf16[2048,80]{1,0:T(8,128)(2,1)S(1)}, bf16[2048,80]{1,0:T(8,128)(2,1)S(1)}, u32[]{:S(2)}, u32[]{:S(2)}) %collective-permute-start.2) | collective-permute-done | bytes 327712 | tf_op jit(solution)/shard_map/ppermute | solution.py:16
  142.9 8.4 %collective-permute-done.4 = bf16[2048,80]{1,0:T(8,128)(2,1)S(1)} collective-permute-done((bf16[2048,80]{1,0:T(8,128)(2,1)S(1)}, bf16[2048,80]{1,0:T(8,128)(2,1)S(1)}, u32[]{:S(2)}, u32[]{:S(2)}) %collective-permute-start.4) | collective-permute-done | bytes 327712 | tf_op jit(solution)/shard_map/ppermute | solution.py:16
  157.8 7.5 %collective-permute-done.6 = bf16[2048,80]{1,0:T(8,128)(2,1)S(1)} collective-permute-done((bf16[2048,80]{1,0:T(8,128)(2,1)S(1)}, bf16[2048,80]{1,0:T(8,128)(2,1)S(1)}, u32[]{:S(2)}, u32[]{:S(2)}) %collective-permute-start.6) | collective-permute-done | bytes 327712 | tf_op jit(solution)/shard_map/ppermute | solution.py:16
  171.9 6.6 %collective-permute-done.8 = bf16[2048,80]{1,0:T(8,128)(2,1)S(1)} collective-permute-done((bf16[2048,80]{1,0:T(8,128)(2,1)S(1)}, bf16[2048,80]{1,0:T(8,128)(2,1)S(1)}, u32[]{:S(2)}, u32[]{:S(2)}) %collective-permute-start.8) | collective-permute-done | bytes 327712 | tf_op jit(solution)/shard_map/ppermute | solution.py:16
  212.3 5.9 %dynamic_update_slice.49 = bf16[2048,1280]{1,0:T(8,128)(2,1)} dynamic-update-slice(bf16[2048,1280]{1,0:T(8,128)(2,1)} %dynamic_update_slice.48, bf16[2048,80]{1,0:T(8,128)(2,1)S(1)} %collective-permute-done, s32[]{:T(128)} %constant.124.clone.1, s32[]{:T(128)S(6)} %select_n.126) | dynamic-update-slice | bytes 655364 | tf_op jit(solution)/shard_map/dynamic_update_slice | solution.py:17
  218.2 6.5 %dynamic_update_slice.50 = bf16[2048,1280]{1,0:T(8,128)(2,1)} dynamic-update-slice(bf16[2048,1280]{1,0:T(8,128)(2,1)} %dynamic_update_slice.49, bf16[2048,80]{1,0:T(8,128)(2,1)S(1)} %collective-permute-done.1, s32[]{:T(128)} %constant.124.clone.1, s32[]{:T(128)S(6)} %select_n.128) | dynamic-update-slice | bytes 655364 | tf_op jit(solution)/shard_map/dynamic_update_slice | solution.py:20
  224.8 6.5 %dynamic_update_slice.51 = bf16[2048,1280]{1,0:T(8,128)(2,1)} dynamic-update-slice(bf16[2048,1280]{1,0:T(8,128)(2,1)} %dynamic_update_slice.50, bf16[2048,80]{1,0:T(8,128)(2,1)S(1)} %collective-permute-done.2, s32[]{:T(128)} %constant.124.clone.1, s32[]{:T(128)S(6)} %select_n.130) | dynamic-update-slice | bytes 655364 | tf_op jit(solution)/shard_map/dynamic_update_slice | solution.py:17
  231.3 6.6 %dynamic_update_slice.52 = bf16[2048,1280]{1,0:T(8,128)(2,1)} dynamic-update-slice(bf16[2048,1280]{1,0:T(8,128)(2,1)} %dynamic_update_slice.51, bf16[2048,80]{1,0:T(8,128)(2,1)S(1)} %collective-permute-done.3, s32[]{:T(128)} %constant.124.clone.1, s32[]{:T(128)S(6)} %select_n.132) | dynamic-update-slice | bytes 655364 | tf_op jit(solution)/shard_map/dynamic_update_slice | solution.py:20
  237.9 6.5 %dynamic_update_slice.53 = bf16[2048,1280]{1,0:T(8,128)(2,1)} dynamic-update-slice(bf16[2048,1280]{1,0:T(8,128)(2,1)} %dynamic_update_slice.52, bf16[2048,80]{1,0:T(8,128)(2,1)S(1)} %collective-permute-done.4, s32[]{:T(128)} %constant.124.clone.1, s32[]{:T(128)S(6)} %select_n.134) | dynamic-update-slice | bytes 655364 | tf_op jit(solution)/shard_map/dynamic_update_slice | solution.py:17
  244.4 6.6 %dynamic_update_slice.54 = bf16[2048,1280]{1,0:T(8,128)(2,1)} dynamic-update-slice(bf16[2048,1280]{1,0:T(8,128)(2,1)} %dynamic_update_slice.53, bf16[2048,80]{1,0:T(8,128)(2,1)S(1)} %copy-done.1, s32[]{:T(128)} %constant.124.clone.1, s32[]{:T(128)S(6)} %select_n.136) | dynamic-update-slice | bytes 655364 | tf_op jit(solution)/shard_map/dynamic_update_slice | solution.py:20
  250.9 6.5 %dynamic_update_slice.55 = bf16[2048,1280]{1,0:T(8,128)(2,1)} dynamic-update-slice(bf16[2048,1280]{1,0:T(8,128)(2,1)} %dynamic_update_slice.54, bf16[2048,80]{1,0:T(8,128)(2,1)S(1)} %copy-done.3, s32[]{:T(128)} %constant.124.clone.1, s32[]{:T(128)S(6)} %select_n.138) | dynamic-update-slice | bytes 655364 | tf_op jit(solution)/shard_map/dynamic_update_slice | solution.py:17
  257.4 6.5 %dynamic_update_slice.56 = bf16[2048,1280]{1,0:T(8,128)(2,1)} dynamic-update-slice(bf16[2048,1280]{1,0:T(8,128)(2,1)} %dynamic_update_slice.55, bf16[2048,80]{1,0:T(8,128)(2,1)S(1)} %copy-done.5, s32[]{:T(128)} %constant.124.clone.1, s32[]{:T(128)S(6)} %select_n.140) | dynamic-update-slice | bytes 655364 | tf_op jit(solution)/shard_map/dynamic_update_slice | solution.py:20
  264.0 6.5 %dynamic_update_slice.57 = bf16[2048,1280]{1,0:T(8,128)(2,1)} dynamic-update-slice(bf16[2048,1280]{1,0:T(8,128)(2,1)} %dynamic_update_slice.56, bf16[2048,80]{1,0:T(8,128)(2,1)S(1)} %copy-done.7, s32[]{:T(128)} %constant.124.clone.1, s32[]{:T(128)S(6)} %select_n.142) | dynamic-update-slice | bytes 655364 | tf_op jit(solution)/shard_map/dynamic_update_slice | solution.py:17
  270.5 6.5 %dynamic_update_slice.58 = bf16[2048,1280]{1,0:T(8,128)(2,1)} dynamic-update-slice(bf16[2048,1280]{1,0:T(8,128)(2,1)} %dynamic_update_slice.57, bf16[2048,80]{1,0:T(8,128)(2,1)S(1)} %copy-done.9, s32[]{:T(128)} %constant.124.clone.1, s32[]{:T(128)S(6)} %select_n.144) | dynamic-update-slice | bytes 655364 | tf_op jit(solution)/shard_map/dynamic_update_slice | solution.py:20
  277.0 6.5 %dynamic_update_slice.59 = bf16[2048,1280]{1,0:T(8,128)(2,1)} dynamic-update-slice(bf16[2048,1280]{1,0:T(8,128)(2,1)} %dynamic_update_slice.58, bf16[2048,80]{1,0:T(8,128)(2,1)S(1)} %copy-done.11, s32[]{:T(128)} %constant.124.clone.1, s32[]{:T(128)S(6)} %select_n.146) | dynamic-update-slice | bytes 655364 | tf_op jit(solution)/shard_map/dynamic_update_slice | solution.py:17
  283.5 6.8 %dynamic_update_slice.60 = bf16[2048,1280]{1,0:T(8,128)(2,1)} dynamic-update-slice(bf16[2048,1280]{1,0:T(8,128)(2,1)} %dynamic_update_slice.59, bf16[2048,80]{1,0:T(8,128)(2,1)} %collective-permute-done.11, s32[]{:T(128)} %constant.124.clone.1, s32[]{:T(128)S(6)} %select_n.148) | dynamic-update-slice | bytes 655364 | tf_op jit(solution)/shard_map/dynamic_update_slice | solution.py:20
  290.3 6.8 %dynamic_update_slice.61 = bf16[2048,1280]{1,0:T(8,128)(2,1)} dynamic-update-slice(bf16[2048,1280]{1,0:T(8,128)(2,1)} %dynamic_update_slice.60, bf16[2048,80]{1,0:T(8,128)(2,1)} %collective-permute-done.12, s32[]{:T(128)} %constant.124.clone.1, s32[]{:T(128)S(6)} %select_n.150) | dynamic-update-slice | bytes 655364 | tf_op jit(solution)/shard_map/dynamic_update_slice | solution.py:17
  297.1 6.8 %dynamic_update_slice.62 = bf16[2048,1280]{1,0:T(8,128)(2,1)} dynamic-update-slice(bf16[2048,1280]{1,0:T(8,128)(2,1)} %dynamic_update_slice.61, bf16[2048,80]{1,0:T(8,128)(2,1)} %collective-permute-done.13, s32[]{:T(128)} %constant.124.clone.1, s32[]{:T(128)S(6)} %select_n.152) | dynamic-update-slice | bytes 655364 | tf_op jit(solution)/shard_map/dynamic_update_slice | solution.py:20
  304.0 6.0 %dynamic_update_slice.63 = bf16[2048,1280]{1,0:T(8,128)(2,1)} dynamic-update-slice(bf16[2048,1280]{1,0:T(8,128)(2,1)} %dynamic_update_slice.62, bf16[2048,80]{1,0:T(8,128)(2,1)} %collective-permute-done.14, s32[]{:T(128)} %constant.124.clone.1, s32[]{:T(128)S(6)} %select_n.154) | dynamic-update-slice | bytes 655364 | tf_op jit(solution)/shard_map/dynamic_update_slice | solution.py:17
  310.0 9.3 %fusion = f32[1280,640]{1,0:T(8,128)} fusion(bf16[2048,1280]{1,0:T(8,128)(2,1)} %dynamic_update_slice.63, bf16[2048,640]{0,1:T(8,128)(2,1)} %all-gather.2.cloned.1.call-done), kind=kOutput, calls=%fused_computation.6 | convolution fusion | flops 3355443200 | bytes 11141120 | tf_op jit(solution)/shard_map/dot_general | solution.py:57
  319.4 96.1 %all-reduce.2.cloned.1.call-done = f32[1280,640]{1,0:T(8,128)} async-done(((f32[1280,640]{1,0:T(8,128)}), f32[1280,640]{1,0:T(8,128)}) %all-reduce.2.cloned.1.call-update) | async-done | bytes 3276816 | tf_op jit(solution)/shard_map/psum | solution.py:66
  (68 shorter events, 74.5 us)
Async XLA Ops:
  6.5 303.4 %all-gather.2.cloned.1.call-start = ((), (), s32[]{:S(2)}) async-start(), calls=%async_computation.2 | async-start | bytes 2949120 | tf_op jit(solution)/shard_map/all_gather | solution.py:56
  63.0 352.5 %all-reduce.2.cloned.1.call-start = ((), (), s32[]{:S(2)}) async-start(), calls=%async_computation.3 | async-start | bytes 6553600 | tf_op jit(solution)/shard_map/psum | solution.py:66
  103.8 16.7 %collective-permute-start = (bf16[2048,80]{1,0:T(8,128)(2,1)S(1)}, bf16[2048,80]{1,0:T(8,128)(2,1)S(1)}, u32[]{:S(2)}, u32[]{:S(2)}) collective-permute-start(bf16[2048,80]{1,0:T(8,128)(2,1)S(1)} %bitcast.15), channel_id=1, source_target_pairs={{0,4},{4,8},{8,12},{12,16},{16,20},{20,24},{24,28},{28,32},{32,36}... | collective-permute-start | bytes 983048 | tf_op jit(solution)/shard_map/ppermute | solution.py:16
  107.9 15.8 %collective-permute-start.1 = (bf16[2048,80]{1,0:T(8,128)(2,1)S(1)}, bf16[2048,80]{1,0:T(8,128)(2,1)S(1)}, u32[]{:S(2)}, u32[]{:S(2)}) collective-permute-start(bf16[2048,80]{1,0:T(8,128)(2,1)S(1)} %bitcast.16), channel_id=1, source_target_pairs={{0,60},{4,0},{8,4},{12,8},{16,12},{20,16},{24,20},{28,24},{32,28},... | collective-permute-start | bytes 983048 | tf_op jit(solution)/shard_map/ppermute | solution.py:19
  120.5 15.9 %collective-permute-start.2 = (bf16[2048,80]{1,0:T(8,128)(2,1)S(1)}, bf16[2048,80]{1,0:T(8,128)(2,1)S(1)}, u32[]{:S(2)}, u32[]{:S(2)}) collective-permute-start(bf16[2048,80]{1,0:T(8,128)(2,1)S(1)} %collective-permute-done), channel_id=1, source_target_pairs={{0,4},{4,8},{8,12},{12,16},{16,20},{20,24},{24,28},{28,32},{32,36}... | collective-permute-start | bytes 983048 | tf_op jit(solution)/shard_map/ppermute | solution.py:16
  123.8 15.0 %collective-permute-start.3 = (bf16[2048,80]{1,0:T(8,128)(2,1)S(1)}, bf16[2048,80]{1,0:T(8,128)(2,1)S(1)}, u32[]{:S(2)}, u32[]{:S(2)}) collective-permute-start(bf16[2048,80]{1,0:T(8,128)(2,1)S(1)} %collective-permute-done.1), channel_id=1, source_target_pairs={{0,60},{4,0},{8,4},{12,8},{16,12},{20,16},{24,20},{28,24},{32,28},... | collective-permute-start | bytes 983048 | tf_op jit(solution)/shard_map/ppermute | solution.py:19
  136.4 14.9 %collective-permute-start.4 = (bf16[2048,80]{1,0:T(8,128)(2,1)S(1)}, bf16[2048,80]{1,0:T(8,128)(2,1)S(1)}, u32[]{:S(2)}, u32[]{:S(2)}) collective-permute-start(bf16[2048,80]{1,0:T(8,128)(2,1)S(1)} %collective-permute-done.2), channel_id=1, source_target_pairs={{0,4},{4,8},{8,12},{12,16},{16,20},{20,24},{24,28},{28,32},{32,36}... | collective-permute-start | bytes 983048 | tf_op jit(solution)/shard_map/ppermute | solution.py:16
  138.8 14.5 %collective-permute-start.5 = (bf16[2048,80]{1,0:T(8,128)(2,1)S(1)}, bf16[2048,80]{1,0:T(8,128)(2,1)S(1)}, u32[]{:S(2)}, u32[]{:S(2)}) collective-permute-start(bf16[2048,80]{1,0:T(8,128)(2,1)S(1)} %collective-permute-done.3), channel_id=1, source_target_pairs={{0,60},{4,0},{8,4},{12,8},{16,12},{20,16},{24,20},{28,24},{32,28},... | collective-permute-start | bytes 983048 | tf_op jit(solution)/shard_map/ppermute | solution.py:19
  151.3 14.0 %collective-permute-start.6 = (bf16[2048,80]{1,0:T(8,128)(2,1)S(1)}, bf16[2048,80]{1,0:T(8,128)(2,1)S(1)}, u32[]{:S(2)}, u32[]{:S(2)}) collective-permute-start(bf16[2048,80]{1,0:T(8,128)(2,1)S(1)} %collective-permute-done.4), channel_id=1, source_target_pairs={{0,4},{4,8},{8,12},{12,16},{16,20},{20,24},{24,28},{28,32},{32,36}... | collective-permute-start | bytes 983048 | tf_op jit(solution)/shard_map/ppermute | solution.py:16
  153.2 12.1 %copy-start = (bf16[2048,80]{1,0:T(8,128)(2,1)}, bf16[2048,80]{1,0:T(8,128)(2,1)S(1)}, u32[]{:S(2)}) copy-start(bf16[2048,80]{1,0:T(8,128)(2,1)S(1)} %collective-permute-done.5) | copy-start | bytes 983044
  153.3 14.0 %collective-permute-start.7 = (bf16[2048,80]{1,0:T(8,128)(2,1)S(1)}, bf16[2048,80]{1,0:T(8,128)(2,1)S(1)}, u32[]{:S(2)}, u32[]{:S(2)}) collective-permute-start(bf16[2048,80]{1,0:T(8,128)(2,1)S(1)} %collective-permute-done.5), channel_id=1, source_target_pairs={{0,60},{4,0},{8,4},{12,8},{16,12},{20,16},{24,20},{28,24},{32,28},... | collective-permute-start | bytes 983048 | tf_op jit(solution)/shard_map/ppermute | solution.py:19
  165.3 13.1 %collective-permute-start.8 = (bf16[2048,80]{1,0:T(8,128)(2,1)S(1)}, bf16[2048,80]{1,0:T(8,128)(2,1)S(1)}, u32[]{:S(2)}, u32[]{:S(2)}) collective-permute-start(bf16[2048,80]{1,0:T(8,128)(2,1)S(1)} %collective-permute-done.6), channel_id=1, source_target_pairs={{0,4},{4,8},{8,12},{12,16},{16,20},{20,24},{24,28},{28,32},{32,36}... | collective-permute-start | bytes 983048 | tf_op jit(solution)/shard_map/ppermute | solution.py:16
  167.3 13.1 %collective-permute-start.9 = (bf16[2048,80]{1,0:T(8,128)(2,1)S(1)}, bf16[2048,80]{1,0:T(8,128)(2,1)S(1)}, u32[]{:S(2)}, u32[]{:S(2)}) collective-permute-start(bf16[2048,80]{1,0:T(8,128)(2,1)S(1)} %collective-permute-done.7), channel_id=1, source_target_pairs={{0,60},{4,0},{8,4},{12,8},{16,12},{20,16},{24,20},{28,24},{32,28},... | collective-permute-start | bytes 983048 | tf_op jit(solution)/shard_map/ppermute | solution.py:19
  178.4 12.2 %collective-permute-start.10 = (bf16[2048,80]{1,0:T(8,128)(2,1)S(1)}, bf16[2048,80]{1,0:T(8,128)(2,1)S(1)}, u32[]{:S(2)}, u32[]{:S(2)}) collective-permute-start(bf16[2048,80]{1,0:T(8,128)(2,1)S(1)} %collective-permute-done.8), channel_id=1, source_target_pairs={{0,4},{4,8},{8,12},{12,16},{16,20},{20,24},{24,28},{28,32},{32,36}... | collective-permute-start | bytes 983048 | tf_op jit(solution)/shard_map/ppermute | solution.py:16
  180.4 12.1 %collective-permute-start.11 = (bf16[2048,80]{1,0:T(8,128)(2,1)S(1)}, bf16[2048,80]{1,0:T(8,128)(2,1)}, u32[]{:S(2)}, u32[]{:S(2)}) collective-permute-start(bf16[2048,80]{1,0:T(8,128)(2,1)S(1)} %collective-permute-done.9), channel_id=1, source_target_pairs={{0,60},{4,0},{8,4},{12,8},{16,12},{20,16},{24,20},{28,24},{32,28},... | collective-permute-start | bytes 983048 | tf_op jit(solution)/shard_map/ppermute | solution.py:19
  190.6 11.2 %collective-permute-start.12 = (bf16[2048,80]{1,0:T(8,128)(2,1)S(1)}, bf16[2048,80]{1,0:T(8,128)(2,1)}, u32[]{:S(2)}, u32[]{:S(2)}) collective-permute-start(bf16[2048,80]{1,0:T(8,128)(2,1)S(1)} %collective-permute-done.10), channel_id=1, source_target_pairs={{0,4},{4,8},{8,12},{12,16},{16,20},{20,24},{24,28},{28,32},{32,36}... | collective-permute-start | bytes 983048 | tf_op jit(solution)/shard_map/ppermute | solution.py:16
  192.5 104.6 %collective-permute-start.13 = (bf16[2048,80]{1,0:T(8,128)(2,1)}, bf16[2048,80]{1,0:T(8,128)(2,1)}, u32[]{:S(2)}, u32[]{:S(2)}) collective-permute-start(bf16[2048,80]{1,0:T(8,128)(2,1)} %collective-permute-done.11), channel_id=1, source_target_pairs={{0,60},{4,0},{8,4},{12,8},{16,12},{20,16},{24,20},{28,24},{32,28},... | collective-permute-start | bytes 983048 | tf_op jit(solution)/shard_map/ppermute | solution.py:19
  201.8 102.1 %collective-permute-start.14 = (bf16[2048,80]{1,0:T(8,128)(2,1)}, bf16[2048,80]{1,0:T(8,128)(2,1)}, u32[]{:S(2)}, u32[]{:S(2)}) collective-permute-start(bf16[2048,80]{1,0:T(8,128)(2,1)} %collective-permute-done.12), channel_id=1, source_target_pairs={{0,4},{4,8},{8,12},{12,16},{16,20},{20,24},{24,28},{28,32},{32,36}... | collective-permute-start | bytes 983048 | tf_op jit(solution)/shard_map/ppermute | solution.py:16
  212.3 32.0 %copy-start.1 = (bf16[2048,80]{1,0:T(8,128)(2,1)S(1)}, bf16[2048,80]{1,0:T(8,128)(2,1)}, u32[]{:S(2)}) copy-start(bf16[2048,80]{1,0:T(8,128)(2,1)} %copy-done) | copy-start | bytes 983044
  218.2 32.7 %copy-start.3 = (bf16[2048,80]{1,0:T(8,128)(2,1)S(1)}, bf16[2048,80]{1,0:T(8,128)(2,1)}, u32[]{:S(2)}) copy-start(bf16[2048,80]{1,0:T(8,128)(2,1)} %copy-done.2) | copy-start | bytes 983044
  224.8 32.7 %copy-start.5 = (bf16[2048,80]{1,0:T(8,128)(2,1)S(1)}, bf16[2048,80]{1,0:T(8,128)(2,1)}, u32[]{:S(2)}) copy-start(bf16[2048,80]{1,0:T(8,128)(2,1)} %copy-done.4) | copy-start | bytes 983044
  231.3 32.7 %copy-start.7 = (bf16[2048,80]{1,0:T(8,128)(2,1)S(1)}, bf16[2048,80]{1,0:T(8,128)(2,1)}, u32[]{:S(2)}) copy-start(bf16[2048,80]{1,0:T(8,128)(2,1)} %copy-done.6) | copy-start | bytes 983044
  237.8 32.6 %copy-start.9 = (bf16[2048,80]{1,0:T(8,128)(2,1)S(1)}, bf16[2048,80]{1,0:T(8,128)(2,1)}, u32[]{:S(2)}) copy-start(bf16[2048,80]{1,0:T(8,128)(2,1)} %copy-done.8) | copy-start | bytes 983044
  244.4 32.6 %copy-start.11 = (bf16[2048,80]{1,0:T(8,128)(2,1)S(1)}, bf16[2048,80]{1,0:T(8,128)(2,1)}, u32[]{:S(2)}) copy-start(bf16[2048,80]{1,0:T(8,128)(2,1)} %copy-done.10) | copy-start | bytes 983044
  (5 other events, 27.2 us)
Sparse Core Ops, SparseCore 0:
  63.1 29.0 all-gather.1
  319.5 95.9 all-reduce.1
